TPU v7x, 32 devices: a whole 2x2x4 slice. The times are simulated.
32 devices in a mesh: rows: 4 (over y, core), feat: 8 (over z, x).
Axes of the slice: x: 2, y: 2, z: 4, core: 2. Of those that a mesh axis runs over, the one named last changes fastest.
Arguments:
- margins: float32 [12288, 32], P(('rows', 'feat')), may hold values from -30 to 260
- labels: int32 [12288], P(('rows', 'feat')), may hold values from 0 to 31
- row_bins: int32 [1024, 12288], P('feat', 'rows'), may hold values from 0 to 63
- parents: int32 [12288], P('rows'), may hold values from 0 to 7
- split_feature: int32 [8], replicated, may hold values from 0 to 1023
- split_bin: int32 [8], replicated, may hold values from 16 to 47
- leaf_values: float32 [16, 32], replicated, may hold values from -4 to 4
Outputs:
- split_gains: float32 [16, 1024, 64], P('rows', 'feat')
- node_totals: float32 [16, 64], replicated
All inputs are finite; a program needn't handle non-finite values.
Results may differ from a plain program's by a relative error of at most 0.0017.
Values may be sent and summed in bfloat16 or wider, within the bound.
No kernel may reach another device: no remote copies, remote signals or barrier semaphores. Data moves between devices by JAX's collectives and lax.ppermute only.
A program may use at most 192 MiB of HBM per device.

v0:
```python
import jax
import jax.numpy as jnp
from jax import lax
from jax.sharding import PartitionSpec as P

BINS = 64
hess_ridge = 1.0


def prefix(value, axis, join, neutral):
    count, mine = (lax.axis_size(axis), lax.axis_index(axis))
    pieces = lax.all_gather(value, axis)
    subtotal = jnp.full_like(value, 0) + jnp.asarray(neutral, value.dtype)

    def turn(position, subtotal):
        longer = join(subtotal, pieces[position])
        return jnp.where(position < mine, longer, subtotal)

    return lax.fori_loop(0, count - 1, turn, subtotal)


def gain_scores(left_sums, totals, classes):
    grad_left = left_sums[..., :classes]
    hess_left = left_sums[..., classes:]
    grad_whole = totals[..., :classes]
    hess_whole = totals[..., classes:]
    grad_right = grad_whole - grad_left
    hess_right = hess_whole - hess_left
    score = (
        grad_left * grad_left / (hess_left + hess_ridge)
        + grad_right * grad_right / (hess_right + hess_ridge)
        - grad_whole * grad_whole / (hess_whole + hess_ridge)
    )
    return jnp.mean(score, axis=-1)


def add_terms(earlier, later):
    return earlier + later


def body(margins, labels, row_bins, parents, split_feature, split_bin, leaf_values):
    feat_dev, group_rows = row_bins.shape
    classes = margins.shape[1]
    node_count = leaf_values.shape[0]
    parent_count = split_feature.shape[0]
    bin_count = BINS
    feat_size = lax.axis_size("feat")
    feat_index = lax.axis_index("feat")
    own_rows = group_rows // feat_size
    parent_hot = parents[:, None] == jnp.arange(parent_count, dtype=jnp.int32)[None, :]
    row_feature = jnp.sum(jnp.where(parent_hot, split_feature[None, :], 0), axis=1)
    row_threshold = jnp.sum(jnp.where(parent_hot, split_bin[None, :], 0), axis=1)
    local_column = row_feature - feat_index * feat_dev
    column_hot = local_column[None, :] == jnp.arange(feat_dev, dtype=jnp.int32)[:, None]
    is_owned = jnp.any(column_hot, axis=0)
    chosen = jnp.sum(jnp.where(column_hot, row_bins, 0), axis=0)
    right_part = jnp.where(is_owned & (chosen > row_threshold), 1.0, 0.0).astype(jnp.float32)
    right_all = lax.psum(right_part.astype(jnp.bfloat16), "feat").astype(jnp.float32)
    node_all = 2 * parents + (right_all > 0.5).astype(jnp.int32)
    node_own = lax.dynamic_slice_in_dim(node_all, feat_index * own_rows, own_rows)
    node_hot_own = (node_own[:, None] == jnp.arange(node_count, dtype=jnp.int32)[None, :]).astype(
        jnp.float32
    )
    logits = margins + jnp.dot(node_hot_own, leaf_values, precision=lax.Precision.HIGHEST)
    probabilities = jax.nn.softmax(logits, axis=1)
    label_hot = (labels[:, None] == jnp.arange(classes, dtype=jnp.int32)[None, :]).astype(
        jnp.float32
    )
    gradient = probabilities - label_hot
    hessian = 2.0 * probabilities * (1.0 - probabilities)
    grad_hess = jnp.concatenate([gradient, hessian], axis=1).astype(jnp.bfloat16)
    partial_totals = lax.dot_general(
        node_hot_own.astype(jnp.bfloat16),
        grad_hess,
        (((0,), (0,)), ((), ())),
        preferred_element_type=jnp.float32,
    )
    node_totals = lax.psum(partial_totals, ("rows", "feat"))
    grad_all = lax.all_gather(grad_hess, "feat", axis=0, tiled=True)
    row_size = lax.axis_size("rows")
    node_hot = node_all[:, None] == jnp.arange(node_count, dtype=jnp.int32)[None, :]
    weighted = jnp.where(node_hot[:, :, None], grad_all[:, None, :], jnp.zeros((), jnp.bfloat16))
    flat_weighted = weighted.reshape(group_rows, node_count * 2 * classes)
    own_bins = bin_count // row_size
    span_rows = own_bins * feat_dev * lax.axis_size("rows")
    bin_span = span_rows // feat_dev
    bin_group = 8

    def one_group(offset):
        values = offset + jnp.arange(bin_group, dtype=jnp.int32)
        one_hot = (row_bins[None, :, :] == values[:, None, None]).astype(jnp.bfloat16)
        one_hot = one_hot.reshape(bin_group * feat_dev, group_rows)
        return jnp.dot(one_hot, flat_weighted, preferred_element_type=jnp.float32)

    blocks = lax.map(one_group, jnp.arange(0, bin_span, bin_group, dtype=jnp.int32))
    own_hist = lax.psum_scatter(
        blocks.reshape(span_rows, node_count * 2 * classes), "rows", scatter_dimension=0, tiled=True
    )
    shaped = own_hist.reshape(own_bins, feat_dev, node_count, 2 * classes)
    running = jnp.cumsum(shaped, axis=0)
    before = prefix(running[-1], "rows", add_terms, jnp.zeros_like(running[-1]))
    left_sums = running + before[None]
    gains_here = gain_scores(left_sums, node_totals[None, None], classes)
    gains_moved = jnp.transpose(gains_here, (2, 1, 0))
    split_gains = lax.all_to_all(gains_moved, "rows", split_axis=0, concat_axis=2, tiled=True)
    return (split_gains, node_totals)


def solution(mesh):
    return jax.shard_map(
        body,
        mesh=mesh,
        in_specs=(
            P(("rows", "feat"), None),
            P(("rows", "feat")),
            P("feat", "rows"),
            P("rows"),
            P(),
            P(),
            P(),
        ),
        out_specs=(P("rows", "feat", None), P()),
        check_vma=False,
    )
```

profile of v0, /device:TPU:0, one launch (start us, length us, event | category | flops | bytes accessed | tf_op | source)
XLA Modules:
  0.0 532.2 jit_solution(12949149705158159860)
XLA Ops:
  7.3 0.8 select_reduce_fusion.1
  8.3 1.6 select_reduce_fusion
  9.9 23.4 %psum.14 = bf16[3072]{0:T(1024)(128)(2,1)S(1)} all-reduce(bf16[3072]{0:T(1024)(128)(2,1)S(1)} %select_convert_fusion), channel_id=1, replica_groups=mesh['rows'=4,'feat'=8] {'feat'}, use_global_device_ids=true, to_apply=%region_4.5 | all-reduce | flops 3072 | bytes 12288 | tf_op jit(solution)/shard_map/psum | solution.py:58
  33.3 0.7 convert_add_fusion
  34.2 1.1 fusion.10
  35.3 0.7 subtract_convert_fusion
  36.1 31.2 %all_gather.6 = bf16[3072,64]{0,1:T(8,128)(2,1)S(1)} all-gather(bf16[384,64]{0,1:T(8,128)(2,1)S(1)} %pad_maximum_fusion), channel_id=1, replica_groups=mesh['rows'=4,'feat'=8] {'feat'}, dimensions={0}, use_global_device_ids=true | all-gather | bytes 442368 | tf_op jit(solution)/shard_map/all_gather | solution.py:79
  67.2 108.7 %while.25 = (s32[]{:T(128)}, f32[8,1024,1024]{2,1,0:T(8,128)}, s32[128,3072]{1,0:T(8,128)}, s32[8]{0:T(128)S(1)}, bf16[3072,64]{0,1:T(8,128)(2,1)S(1)}, /*index=5*/pred[3072,16]{0,1:T(8,128)(4,1)S(1)}, s32[]{:T(128)}) while((s32[]{:T(128)}, f32[8,1024,1024]{2,1,0:T(8,128)}, s32[128,3072]{1,0:T(8,128)}, s32[8]{0:T(128)S(1)}, ...), condition=%wide.region_8.9_spmd.clone, body=%wide.region_7.8_spmd.clone.sunk | while | flops 6448742400 | bytes 25092764 | solution.py:95
  67.2 0.6 dynamic_slice.20
  67.8 0.6 iota_add_fusion.2
  68.5 3.4 bitcast_compare_fusion.2
  72.5 8.3 %bitcast_dynamic-update-slice_fusion.2 = f32[8,1024,1024]{2,1,0:T(8,128)} fusion(f32[8,1024,1024]{2,1,0:T(8,128)} %get-tuple-element.270, s32[]{:T(128)} %get-tuple-element.269, pred[1024,3072]{1,0:T(32,128)(4,1)S(1)} %bitcast_compare_fusion.2, bf16[3072,1024]{0,1:T(8,128)(2,1)S(1)} %bitcast.48), kind=kOutput, calls=%fused_computation.3.clone.1 | convolution fusion | flops 6442450944 | bytes 13632000 | tf_op jit(solution)/shard_map/while/body/eval_jaxpr/dot_general | solution.py:93
  81.4 0.6 iota_add_fusion.2
  82.2 3.4 bitcast_compare_fusion.2
  86.2 8.3 %bitcast_dynamic-update-slice_fusion.2 = f32[8,1024,1024]{2,1,0:T(8,128)} fusion(f32[8,1024,1024]{2,1,0:T(8,128)} %get-tuple-element.270, s32[]{:T(128)} %get-tuple-element.269, pred[1024,3072]{1,0:T(32,128)(4,1)S(1)} %bitcast_compare_fusion.2, bf16[3072,1024]{0,1:T(8,128)(2,1)S(1)} %bitcast.48), kind=kOutput, calls=%fused_computation.3.clone.1 | convolution fusion | flops 6442450944 | bytes 13632000 | tf_op jit(solution)/shard_map/while/body/eval_jaxpr/dot_general | solution.py:93
  95.0 0.6 iota_add_fusion.2
  95.8 3.4 bitcast_compare_fusion.2
  99.7 8.3 %bitcast_dynamic-update-slice_fusion.2 = f32[8,1024,1024]{2,1,0:T(8,128)} fusion(f32[8,1024,1024]{2,1,0:T(8,128)} %get-tuple-element.270, s32[]{:T(128)} %get-tuple-element.269, pred[1024,3072]{1,0:T(32,128)(4,1)S(1)} %bitcast_compare_fusion.2, bf16[3072,1024]{0,1:T(8,128)(2,1)S(1)} %bitcast.48), kind=kOutput, calls=%fused_computation.3.clone.1 | convolution fusion | flops 6442450944 | bytes 13632000 | tf_op jit(solution)/shard_map/while/body/eval_jaxpr/dot_general | solution.py:93
  108.6 0.6 iota_add_fusion.2
  109.3 3.4 bitcast_compare_fusion.2
  113.3 8.3 %bitcast_dynamic-update-slice_fusion.2 = f32[8,1024,1024]{2,1,0:T(8,128)} fusion(f32[8,1024,1024]{2,1,0:T(8,128)} %get-tuple-element.270, s32[]{:T(128)} %get-tuple-element.269, pred[1024,3072]{1,0:T(32,128)(4,1)S(1)} %bitcast_compare_fusion.2, bf16[3072,1024]{0,1:T(8,128)(2,1)S(1)} %bitcast.48), kind=kOutput, calls=%fused_computation.3.clone.1 | convolution fusion | flops 6442450944 | bytes 13632000 | tf_op jit(solution)/shard_map/while/body/eval_jaxpr/dot_general | solution.py:93
  122.2 0.6 iota_add_fusion.2
  122.9 3.4 bitcast_compare_fusion.2
  126.9 8.3 %bitcast_dynamic-update-slice_fusion.2 = f32[8,1024,1024]{2,1,0:T(8,128)} fusion(f32[8,1024,1024]{2,1,0:T(8,128)} %get-tuple-element.270, s32[]{:T(128)} %get-tuple-element.269, pred[1024,3072]{1,0:T(32,128)(4,1)S(1)} %bitcast_compare_fusion.2, bf16[3072,1024]{0,1:T(8,128)(2,1)S(1)} %bitcast.48), kind=kOutput, calls=%fused_computation.3.clone.1 | convolution fusion | flops 6442450944 | bytes 13632000 | tf_op jit(solution)/shard_map/while/body/eval_jaxpr/dot_general | solution.py:93
  135.8 0.6 iota_add_fusion.2
  136.5 3.4 bitcast_compare_fusion.2
  140.5 8.3 %bitcast_dynamic-update-slice_fusion.2 = f32[8,1024,1024]{2,1,0:T(8,128)} fusion(f32[8,1024,1024]{2,1,0:T(8,128)} %get-tuple-element.270, s32[]{:T(128)} %get-tuple-element.269, pred[1024,3072]{1,0:T(32,128)(4,1)S(1)} %bitcast_compare_fusion.2, bf16[3072,1024]{0,1:T(8,128)(2,1)S(1)} %bitcast.48), kind=kOutput, calls=%fused_computation.3.clone.1 | convolution fusion | flops 6442450944 | bytes 13632000 | tf_op jit(solution)/shard_map/while/body/eval_jaxpr/dot_general | solution.py:93
  149.4 0.6 iota_add_fusion.2
  150.1 3.4 bitcast_compare_fusion.2
  154.1 8.3 %bitcast_dynamic-update-slice_fusion.2 = f32[8,1024,1024]{2,1,0:T(8,128)} fusion(f32[8,1024,1024]{2,1,0:T(8,128)} %get-tuple-element.270, s32[]{:T(128)} %get-tuple-element.269, pred[1024,3072]{1,0:T(32,128)(4,1)S(1)} %bitcast_compare_fusion.2, bf16[3072,1024]{0,1:T(8,128)(2,1)S(1)} %bitcast.48), kind=kOutput, calls=%fused_computation.3.clone.1 | convolution fusion | flops 6442450944 | bytes 13632000 | tf_op jit(solution)/shard_map/while/body/eval_jaxpr/dot_general | solution.py:93
  162.9 0.6 iota_add_fusion.2
  163.7 3.4 bitcast_compare_fusion.2
  167.6 8.3 %bitcast_dynamic-update-slice_fusion.2 = f32[8,1024,1024]{2,1,0:T(8,128)} fusion(f32[8,1024,1024]{2,1,0:T(8,128)} %get-tuple-element.270, s32[]{:T(128)} %get-tuple-element.269, pred[1024,3072]{1,0:T(32,128)(4,1)S(1)} %bitcast_compare_fusion.2, bf16[3072,1024]{0,1:T(8,128)(2,1)S(1)} %bitcast.48), kind=kOutput, calls=%fused_computation.3.clone.1 | convolution fusion | flops 6442450944 | bytes 13632000 | tf_op jit(solution)/shard_map/while/body/eval_jaxpr/dot_general | solution.py:93
  175.9 31.1 %copy.51 = f32[8192,1024]{0,1:T(8,128)} copy(f32[8192,1024]{1,0:T(8,128)} %bitcast.49) | data formatting | bytes 67108864 | tf_op jit(solution)/shard_map/reshape | solution.py:97
  207.3 229.4 %reduce-scatter.2.cloned.1.call-done = f32[2048,1024]{0,1:T(8,128)} async-done(((f32[8192,1024]{0,1:T(8,128)}), f32[2048,1024]{0,1:T(8,128)}) %reduce-scatter.2.cloned.1.call-update) | async-done | bytes 8388624 | tf_op jit(solution)/shard_map/reduce_scatter | solution.py:96
  436.7 8.6 %copy.62 = f32[128,8,16,128]{3,2,1,0:T(8,128)} copy(f32[128,8,16,128]{3,1,2,0:T(8,128)} %bitcast.51) | data formatting | bytes 16777216
  445.3 15.0 %fusion.2 = f32[16,128,16,64]{1,2,3,0:T(8,128)} fusion(f32[16,128,16,64]{1,0,3,2:T(8,128)} %bitcast.50), kind=kOutput, calls=%fused_computation.8 | output fusion | flops 31457280 | bytes 16777216 | tf_op jit(solution)/shard_map/jit(cumsum)/reduce_window_sum | solution.py:100
  460.3 1.1 slice.20
  461.4 1.0 copy.53
  462.7 39.9 %psum.15 = f32[16,64]{1,0:T(8,128)S(1)} all-reduce(f32[16,64]{1,0:T(8,128)S(1)} %fusion.5), channel_id=1, replica_groups=mesh['rows'=4,'feat'=8] {'rows','feat'}, use_global_device_ids=true, to_apply=%region_13.14 | all-reduce | flops 1024 | bytes 8192 | tf_op jit(solution)/shard_map/psum | solution.py:78
  503.2 5.8 %while.26 = (s32[]{:T(128)}, f32[128,16,64]{2,1,0:T(8,128)S(1)}, s32[]{:T(128)}, f32[4,128,16,64]{1,3,2,0:T(8,128)}, s32[]{:T(128)}, /*index=5*/s32[]{:T(128)}) while((s32[]{:T(128)}, f32[128,16,64]{2,1,0:T(8,128)S(1)}, s32[]{:T(128)}, f32[4,128,16,64]{1,3,2,0:T(8,128)}, s32[]{:T(128)}, /*index=5*/s32[]{:T(128)}) %tuple.67), condition=%wide.region_12.13_spmd.clone, body=%wide.region_11.12_spmd.clone.sunk | while | flops 393220 | bytes 3670109 | solution.py:19
  503.2 1.1 constant_dynamic-slice_fusion.2
  505.1 1.1 constant_dynamic-slice_fusion.2
  507.0 1.1 constant_dynamic-slice_fusion.2
  509.5 4.4 broadcast_add_fusion
  513.9 2.7 subtract_reduce_fusion
  516.7 8.0 %all_to_all.18 = f32[16,128,16]{1,2,0:T(8,128)S(1)} all-to-all(f32[16,128,16]{1,2,0:T(8,128)S(1)} %copy.59), channel_id=1, replica_groups=mesh['rows'=4,'feat'=8] {'rows'}, dimensions={0} | all-to-all | bytes 262144 | tf_op jit(solution)/shard_map/all_to_all | solution.py:105
  524.7 0.7 copy.60
  (58 shorter events, 13.9 us)
Async XLA Ops:
  7.2 27.0 %copy-start = (f32[16,32]{1,0:T(8,128)S(1)}, f32[16,32]{1,0:T(8,128)}, u32[]{:S(2)}) copy-start(f32[16,32]{1,0:T(8,128)} %param.17) | copy-start | bytes 6148
  7.2 429.5 %reduce-scatter.2.cloned.1.call-start = ((), (), s32[]{:S(2)}) async-start(), calls=%async_computation.2 | async-start | bytes 41943040 | tf_op jit(solution)/shard_map/reduce_scatter | solution.py:96
  207.1 295.8 %all-gather.2.cloned.1.call-start = ((), (), s32[]{:S(2)}) async-start(), calls=%async_computation.3 | async-start | bytes 2621440 | tf_op jit(solution)/shard_map/all_gather | solution.py:12
  502.6 0.6 copy-start.2
  509.5 15.9 %copy-start.1 = (f32[16,32]{1,0:T(8,128)S(1)}, f32[16,32]{1,0:T(8,128)}, u32[]{:S(2)}) copy-start(f32[16,32]{1,0:T(8,128)} %param.17) | copy-start | bytes 6148
Sparse Core Ops, SparseCore 0:
  207.2 229.4 reduce-scatter.1
  462.5 22.7 all-gather.1
where the time goes:
time: 534 us; the launch traced here: 532 us
  waiting for transfers between devices  229 us (43%)
  blocking collectives  102 us (19%)
  matrix products  67.8 us (13%)
  other arithmetic  64.3 us (12%)
  local copies, waits for them, and re-layouts  53.6 us (10%)
  between operations  14.2 us (3%)
    reduce_scatter x1, waiting for transfers between devices, body(): lax.psum_scatter(blocks.reshape(span_rows, node_count * 2 * classes), 'ro...  229 us
    dot_general x8, matrix products, one_group(): return jnp.dot(one_hot, flat_weighted, preferred_element_type=jnp.float32)  66.4 us
    psum x1, blocking collectives, body(): node_totals = lax.psum(partial_totals, ('rows', 'feat'))  39.9 us
    all_gather x1, blocking collectives, body(): grad_all = lax.all_gather(grad_hess, 'feat', axis=0, tiled=True)  31.2 us
    reshape x1, local copies, waits for them, and re-layouts, body(): blocks.reshape(span_rows, node_count * 2 * classes)  31.1 us
    eq x8, other arithmetic, one_group(): row_bins[None, :, :] == values[:, None, None]  27.1 us
    psum x1, blocking collectives, body(): lax.psum(right_part.astype(jnp.bfloat16), 'feat').astype(jnp.float32)  23.4 us
    another operation x1, other arithmetic, body(): running = jnp.cumsum(shaped, axis=0)  15 us
  transfers between devices with their start and end apart: 2, of which 1 were waited for; matrix products, arithmetic and copies ran while one was open for 0% of the time, Pallas kernels for 0%

commit v1 on v0

--- a/solution.py
+++ b/solution.py
@@ -76,7 +76,14 @@
         preferred_element_type=jnp.float32,
     )
     node_totals = lax.psum(partial_totals, ("rows", "feat"))
-    grad_all = lax.all_gather(grad_hess, "feat", axis=0, tiled=True)
+    ways, here = (lax.axis_size("feat"), lax.axis_index("feat"))
+    grad_all, reach = (grad_hess, 1)
+    while reach < ways:
+        theirs = lax.ppermute(grad_all, "feat", [(d, d ^ reach) for d in range(ways)])
+        mine_first = jnp.concatenate([grad_all, theirs], axis=0)
+        theirs_first = jnp.concatenate([theirs, grad_all], axis=0)
+        grad_all = jnp.where(here & reach == 0, mine_first, theirs_first)
+        reach = 2 * reach
     row_size = lax.axis_size("rows")
     node_hot = node_all[:, None] == jnp.arange(node_count, dtype=jnp.int32)[None, :]
     weighted = jnp.where(node_hot[:, :, None], grad_all[:, None, :], jnp.zeros((), jnp.bfloat16))

time: 534 us -> 521 us (0.976)
  blocking collectives: 102 us -> 71.2 us
  waiting for transfers between devices: 229 us -> 248 us
    all_gather x1 -> x0, blocking collectives: 31.2 us -> none  [body(): grad_all = lax.all_gather(grad_hess, 'feat', axis=0, tiled=True)]
    ppermute x0 -> x3, waiting for transfers between devices: none -> 18.3 us  [body(): lax.ppermute(grad_all, 'feat', [(d, d ^ reach) for d in range(ways)])]
  transfers between devices with their start and end apart: 2 -> 5, of which waited for: 1 -> 4; matrix products, arithmetic and copies ran while one was open for 0% -> 0% of each run, Pallas kernels for 0% -> 0%
where the time goes in v1:
time: 521 us; the launch traced here: 520 us
  waiting for transfers between devices  248 us (48%)
  blocking collectives  71.2 us (14%)
  matrix products  67.8 us (13%)
  other arithmetic  64.4 us (12%)
  local copies, waits for them, and re-layouts  53.6 us (10%)
  between operations  14.2 us (3%)
    reduce_scatter x1, waiting for transfers between devices, body(): lax.psum_scatter(blocks.reshape(span_rows, node_count * 2 * classes), 'ro...  229 us
    dot_general x8, matrix products, one_group(): return jnp.dot(one_hot, flat_weighted, preferred_element_type=jnp.float32)  66.4 us
    psum x1, blocking collectives, body(): node_totals = lax.psum(partial_totals, ('rows', 'feat'))  39.9 us
    reshape x1, local copies, waits for them, and re-layouts, body(): blocks.reshape(span_rows, node_count * 2 * classes)  31.1 us
    eq x8, other arithmetic, one_group(): row_bins[None, :, :] == values[:, None, None]  27.1 us
    psum x1, blocking collectives, body(): lax.psum(right_part.astype(jnp.bfloat16), 'feat').astype(jnp.float32)  23.4 us
    ppermute x3, waiting for transfers between devices, body(): lax.ppermute(grad_all, 'feat', [(d, d ^ reach) for d in range(ways)])  18.3 us
    another operation x1, other arithmetic, body(): running = jnp.cumsum(shaped, axis=0)  15 us
  transfers between devices with their start and end apart: 5, of which 4 were waited for; matrix products, arithmetic and copies ran while one was open for 0% of the time, Pallas kernels for 0%

profile of v1, /device:TPU:0, one launch (start us, length us, event | category | flops | bytes accessed | tf_op | source)
XLA Modules:
  0.0 519.7 jit_solution(10273535343297673320)
XLA Ops:
  7.2 0.8 select_reduce_fusion.1
  8.3 1.6 select_reduce_fusion
  9.9 23.4 %psum.14 = bf16[3072]{0:T(1024)(128)(2,1)S(1)} all-reduce(bf16[3072]{0:T(1024)(128)(2,1)S(1)} %select_convert_fusion), channel_id=1, replica_groups=mesh['rows'=4,'feat'=8] {'feat'}, use_global_device_ids=true, to_apply=%region_4.5 | all-reduce | flops 3072 | bytes 12288 | tf_op jit(solution)/shard_map/psum | solution.py:58
  33.3 0.7 convert_add_fusion
  34.1 1.1 fusion.10
  35.3 0.7 subtract_convert_fusion
  36.1 4.1 collective-permute-done
  40.3 6.6 %collective-permute-done.1 = bf16[768,64]{0,1:T(8,128)(2,1)S(1)} collective-permute-done((bf16[768,64]{0,1:T(8,128)(2,1)S(1)}, bf16[768,64]{0,1:T(8,128)(2,1)S(1)}, u32[]{:S(2)}, u32[]{:S(2)}) %collective-permute-start.1) | collective-permute-done | bytes 98336 | tf_op jit(solution)/shard_map/ppermute | solution.py:82
  47.1 7.6 %collective-permute-done.2 = bf16[1536,64]{0,1:T(8,128)(2,1)S(1)} collective-permute-done((bf16[1536,64]{0,1:T(8,128)(2,1)S(1)}, bf16[1536,64]{0,1:T(8,128)(2,1)S(1)}, u32[]{:S(2)}, u32[]{:S(2)}) %collective-permute-start.2) | collective-permute-done | bytes 196640 | tf_op jit(solution)/shard_map/ppermute | solution.py:82
  54.8 108.7 %while.25 = (s32[]{:T(128)}, f32[8,1024,1024]{2,1,0:T(8,128)}, s32[128,3072]{1,0:T(8,128)}, s32[8]{0:T(128)S(1)}, bf16[3072,64]{0,1:T(8,128)(2,1)S(1)}, /*index=5*/pred[3072,16]{0,1:T(8,128)(4,1)S(1)}, s32[]{:T(128)}) while((s32[]{:T(128)}, f32[8,1024,1024]{2,1,0:T(8,128)}, s32[128,3072]{1,0:T(8,128)}, s32[8]{0:T(128)S(1)}, ...), condition=%wide.region_8.9_spmd.clone, body=%wide.region_7.8_spmd.clone.sunk | while | flops 6448742400 | bytes 25092764 | solution.py:102
  55.4 0.6 iota_add_fusion.2
  56.1 3.4 bitcast_compare_fusion.2
  60.1 8.3 %bitcast_dynamic-update-slice_fusion.2 = f32[8,1024,1024]{2,1,0:T(8,128)} fusion(f32[8,1024,1024]{2,1,0:T(8,128)} %get-tuple-element.270, s32[]{:T(128)} %get-tuple-element.269, pred[1024,3072]{1,0:T(32,128)(4,1)S(1)} %bitcast_compare_fusion.2, bf16[3072,1024]{0,1:T(8,128)(2,1)S(1)} %bitcast.48), kind=kOutput, calls=%fused_computation.3.clone.1 | convolution fusion | flops 6442450944 | bytes 13632000 | tf_op jit(solution)/shard_map/while/body/eval_jaxpr/dot_general | solution.py:100
  69.0 0.6 iota_add_fusion.2
  69.7 3.4 bitcast_compare_fusion.2
  73.7 8.3 %bitcast_dynamic-update-slice_fusion.2 = f32[8,1024,1024]{2,1,0:T(8,128)} fusion(f32[8,1024,1024]{2,1,0:T(8,128)} %get-tuple-element.270, s32[]{:T(128)} %get-tuple-element.269, pred[1024,3072]{1,0:T(32,128)(4,1)S(1)} %bitcast_compare_fusion.2, bf16[3072,1024]{0,1:T(8,128)(2,1)S(1)} %bitcast.48), kind=kOutput, calls=%fused_computation.3.clone.1 | convolution fusion | flops 6442450944 | bytes 13632000 | tf_op jit(solution)/shard_map/while/body/eval_jaxpr/dot_general | solution.py:100
  82.6 0.6 iota_add_fusion.2
  83.3 3.4 bitcast_compare_fusion.2
  87.3 8.3 %bitcast_dynamic-update-slice_fusion.2 = f32[8,1024,1024]{2,1,0:T(8,128)} fusion(f32[8,1024,1024]{2,1,0:T(8,128)} %get-tuple-element.270, s32[]{:T(128)} %get-tuple-element.269, pred[1024,3072]{1,0:T(32,128)(4,1)S(1)} %bitcast_compare_fusion.2, bf16[3072,1024]{0,1:T(8,128)(2,1)S(1)} %bitcast.48), kind=kOutput, calls=%fused_computation.3.clone.1 | convolution fusion | flops 6442450944 | bytes 13632000 | tf_op jit(solution)/shard_map/while/body/eval_jaxpr/dot_general | solution.py:100
  96.2 0.6 iota_add_fusion.2
  96.9 3.4 bitcast_compare_fusion.2
  100.9 8.3 %bitcast_dynamic-update-slice_fusion.2 = f32[8,1024,1024]{2,1,0:T(8,128)} fusion(f32[8,1024,1024]{2,1,0:T(8,128)} %get-tuple-element.270, s32[]{:T(128)} %get-tuple-element.269, pred[1024,3072]{1,0:T(32,128)(4,1)S(1)} %bitcast_compare_fusion.2, bf16[3072,1024]{0,1:T(8,128)(2,1)S(1)} %bitcast.48), kind=kOutput, calls=%fused_computation.3.clone.1 | convolution fusion | flops 6442450944 | bytes 13632000 | tf_op jit(solution)/shard_map/while/body/eval_jaxpr/dot_general | solution.py:100
  109.7 0.6 iota_add_fusion.2
  110.5 3.4 bitcast_compare_fusion.2
  114.4 8.3 %bitcast_dynamic-update-slice_fusion.2 = f32[8,1024,1024]{2,1,0:T(8,128)} fusion(f32[8,1024,1024]{2,1,0:T(8,128)} %get-tuple-element.270, s32[]{:T(128)} %get-tuple-element.269, pred[1024,3072]{1,0:T(32,128)(4,1)S(1)} %bitcast_compare_fusion.2, bf16[3072,1024]{0,1:T(8,128)(2,1)S(1)} %bitcast.48), kind=kOutput, calls=%fused_computation.3.clone.1 | convolution fusion | flops 6442450944 | bytes 13632000 | tf_op jit(solution)/shard_map/while/body/eval_jaxpr/dot_general | solution.py:100
  123.4 0.6 iota_add_fusion.2
  124.1 3.4 bitcast_compare_fusion.2
  128.1 8.3 %bitcast_dynamic-update-slice_fusion.2 = f32[8,1024,1024]{2,1,0:T(8,128)} fusion(f32[8,1024,1024]{2,1,0:T(8,128)} %get-tuple-element.270, s32[]{:T(128)} %get-tuple-element.269, pred[1024,3072]{1,0:T(32,128)(4,1)S(1)} %bitcast_compare_fusion.2, bf16[3072,1024]{0,1:T(8,128)(2,1)S(1)} %bitcast.48), kind=kOutput, calls=%fused_computation.3.clone.1 | convolution fusion | flops 6442450944 | bytes 13632000 | tf_op jit(solution)/shard_map/while/body/eval_jaxpr/dot_general | solution.py:100
  137.7 3.4 bitcast_compare_fusion.2
  141.6 8.3 %bitcast_dynamic-update-slice_fusion.2 = f32[8,1024,1024]{2,1,0:T(8,128)} fusion(f32[8,1024,1024]{2,1,0:T(8,128)} %get-tuple-element.270, s32[]{:T(128)} %get-tuple-element.269, pred[1024,3072]{1,0:T(32,128)(4,1)S(1)} %bitcast_compare_fusion.2, bf16[3072,1024]{0,1:T(8,128)(2,1)S(1)} %bitcast.48), kind=kOutput, calls=%fused_computation.3.clone.1 | convolution fusion | flops 6442450944 | bytes 13632000 | tf_op jit(solution)/shard_map/while/body/eval_jaxpr/dot_general | solution.py:100
  150.5 0.6 iota_add_fusion.2
  151.2 3.4 bitcast_compare_fusion.2
  155.2 8.3 %bitcast_dynamic-update-slice_fusion.2 = f32[8,1024,1024]{2,1,0:T(8,128)} fusion(f32[8,1024,1024]{2,1,0:T(8,128)} %get-tuple-element.270, s32[]{:T(128)} %get-tuple-element.269, pred[1024,3072]{1,0:T(32,128)(4,1)S(1)} %bitcast_compare_fusion.2, bf16[3072,1024]{0,1:T(8,128)(2,1)S(1)} %bitcast.48), kind=kOutput, calls=%fused_computation.3.clone.1 | convolution fusion | flops 6442450944 | bytes 13632000 | tf_op jit(solution)/shard_map/while/body/eval_jaxpr/dot_general | solution.py:100
  163.5 31.1 %copy.51 = f32[8192,1024]{0,1:T(8,128)} copy(f32[8192,1024]{1,0:T(8,128)} %bitcast.49) | data formatting | bytes 67108864 | tf_op jit(solution)/shard_map/reshape | solution.py:104
  194.9 229.4 %reduce-scatter.2.cloned.1.call-done = f32[2048,1024]{0,1:T(8,128)} async-done(((f32[8192,1024]{0,1:T(8,128)}), f32[2048,1024]{0,1:T(8,128)}) %reduce-scatter.2.cloned.1.call-update) | async-done | bytes 8388624 | tf_op jit(solution)/shard_map/reduce_scatter | solution.py:103
  424.3 8.6 %copy.62 = f32[128,8,16,128]{3,2,1,0:T(8,128)} copy(f32[128,8,16,128]{3,1,2,0:T(8,128)} %bitcast.51) | data formatting | bytes 16777216
  432.8 15.0 %fusion.2 = f32[16,128,16,64]{1,2,3,0:T(8,128)} fusion(f32[16,128,16,64]{1,0,3,2:T(8,128)} %bitcast.50), kind=kOutput, calls=%fused_computation.8 | output fusion | flops 31457280 | bytes 16777216 | tf_op jit(solution)/shard_map/jit(cumsum)/reduce_window_sum | solution.py:107
  447.8 1.1 slice.20
  448.9 1.0 copy.53
  450.2 39.9 %psum.15 = f32[16,64]{1,0:T(8,128)S(1)} all-reduce(f32[16,64]{1,0:T(8,128)S(1)} %fusion.5), channel_id=1, replica_groups=mesh['rows'=4,'feat'=8] {'rows','feat'}, use_global_device_ids=true, to_apply=%region_13.14 | all-reduce | flops 1024 | bytes 8192 | tf_op jit(solution)/shard_map/psum | solution.py:78
  490.7 5.8 %while.26 = (s32[]{:T(128)}, f32[128,16,64]{2,1,0:T(8,128)S(1)}, s32[]{:T(128)}, f32[4,128,16,64]{1,3,2,0:T(8,128)}, s32[]{:T(128)}, /*index=5*/s32[]{:T(128)}) while((s32[]{:T(128)}, f32[128,16,64]{2,1,0:T(8,128)S(1)}, s32[]{:T(128)}, f32[4,128,16,64]{1,3,2,0:T(8,128)}, s32[]{:T(128)}, /*index=5*/s32[]{:T(128)}) %tuple.67), condition=%wide.region_12.13_spmd.clone, body=%wide.region_11.12_spmd.clone.sunk | while | flops 393220 | bytes 3670109 | solution.py:19
  490.7 1.1 constant_dynamic-slice_fusion.2
  492.6 1.1 constant_dynamic-slice_fusion.2
  494.5 1.1 constant_dynamic-slice_fusion.2
  497.0 4.4 broadcast_add_fusion
  501.4 2.7 subtract_reduce_fusion
  504.2 8.0 %all_to_all.18 = f32[16,128,16]{1,2,0:T(8,128)S(1)} all-to-all(f32[16,128,16]{1,2,0:T(8,128)S(1)} %copy.59), channel_id=1, replica_groups=mesh['rows'=4,'feat'=8] {'rows'}, dimensions={0} | all-to-all | bytes 262144 | tf_op jit(solution)/shard_map/all_to_all | solution.py:112
  512.2 0.7 copy.60
  (66 shorter events, 15.5 us)
Async XLA Ops:
  7.2 26.9 %copy-start = (f32[16,32]{1,0:T(8,128)S(1)}, f32[16,32]{1,0:T(8,128)}, u32[]{:S(2)}) copy-start(f32[16,32]{1,0:T(8,128)} %param.17) | copy-start | bytes 6148
  7.2 417.1 %reduce-scatter.2.cloned.1.call-start = ((), (), s32[]{:S(2)}) async-start(), calls=%async_computation.2 | async-start | bytes 41943040 | tf_op jit(solution)/shard_map/reduce_scatter | solution.py:103
  36.0 4.2 collective-permute-start
  40.2 6.7 %collective-permute-start.1 = (bf16[768,64]{0,1:T(8,128)(2,1)S(1)}, bf16[768,64]{0,1:T(8,128)(2,1)S(1)}, u32[]{:S(2)}, u32[]{:S(2)}) collective-permute-start(bf16[768,64]{0,1:T(8,128)(2,1)S(1)} %maximum_select_fusion.2), channel_id=1, source_target_pairs={{0,2},{1,3},{2,0},{3,1},{4,6},{5,7},{6,4},{7,5},{8,10},{9,11},{10,... | collective-permute-start | bytes 294920 | tf_op jit(solution)/shard_map/ppermute | solution.py:82
  46.9 7.8 %collective-permute-start.2 = (bf16[1536,64]{0,1:T(8,128)(2,1)S(1)}, bf16[1536,64]{0,1:T(8,128)(2,1)S(1)}, u32[]{:S(2)}, u32[]{:S(2)}) collective-permute-start(bf16[1536,64]{0,1:T(8,128)(2,1)S(1)} %maximum_select_fusion.1), channel_id=1, source_target_pairs={{0,4},{1,5},{2,6},{3,7},{4,0},{5,1},{6,2},{7,3},{8,12},{9,13},{10,... | collective-permute-start | bytes 589832 | tf_op jit(solution)/shard_map/ppermute | solution.py:82
  194.6 295.8 %all-gather.2.cloned.1.call-start = ((), (), s32[]{:S(2)}) async-start(), calls=%async_computation.3 | async-start | bytes 2621440 | tf_op jit(solution)/shard_map/all_gather | solution.py:12
  490.1 0.6 copy-start.2
  497.0 15.9 %copy-start.1 = (f32[16,32]{1,0:T(8,128)S(1)}, f32[16,32]{1,0:T(8,128)}, u32[]{:S(2)}) copy-start(f32[16,32]{1,0:T(8,128)} %param.17) | copy-start | bytes 6148
Sparse Core Ops, SparseCore 0:
  194.7 229.4 reduce-scatter.1
  450.1 22.7 all-gather.1
